TPU v7x, 256 devices: a whole 4x4x8 slice. The times are simulated.
256 devices in a mesh: dp: 32 (over x, y, core), type: 8 (over z).
Axes of the slice: x: 4, y: 4, z: 8, core: 2. Of those that a mesh axis runs over, the one named last changes fastest.
Arguments:
- tokens: bfloat16 [32768, 4096], P(('dp', 'type')), may hold values from -6 to 6
- token_types: int32 [32768, 1], P(('dp', 'type')), may hold values from 0 to 7
- tile_mask: int32 [32, 8, 8], P('dp', 'type'), may hold values from 0 to 1, as said below
- queries: bfloat16 [32768, 4096], P(('dp', 'type')), may hold values from -60 to 60
- keys: bfloat16 [32768, 4096], P(('dp', 'type')), may hold values from -4 to 4
- gate_weight: bfloat16 [8, 4096, 7168], P('type', None, 'dp'), may hold values from -0.09375 to 0.09375
- up_weight: bfloat16 [8, 4096, 7168], P('type', None, 'dp'), may hold values from -0.09375 to 0.09375
- down_weight: bfloat16 [8, 7168, 4096], P('type', 'dp'), may hold values from -0.0625 to 0.0625
Outputs:
- expert_out: bfloat16 [32768, 4096], P(('dp', 'type'))
- attended: bfloat16 [32768, 4096], P(('dp', 'type'))
Inputs may be any that keep to these rules, and one draw needn't show every extreme that they name: `tile_mask`: every diagonal entry is 1.
All inputs are finite; a program needn't handle non-finite values.
Results may differ from a plain program's by a relative error of at most 0.02.
Values may be sent and summed in bfloat16 or wider, within the bound.
A program may use at most 128 MiB of HBM per device.

v0:
```python
import math
import jax
import jax.numpy as jnp
from jax import lax
from jax.sharding import PartitionSpec as P

HEAD = 128
EXP_CAP = 16


def on_device(tokens, token_types, tile_mask, queries, keys, gate_weight, up_weight, down_weight):
    n_type = lax.axis_size("type")
    my_index = lax.axis_index("type")
    tok_rows = tokens.shape[0]
    feat_width = tokens.shape[1]
    type_ids = jnp.arange(n_type, dtype=jnp.int32)
    slot_ids = jnp.arange(EXP_CAP, dtype=jnp.int32)
    keys_all = lax.all_gather(keys, "type", axis=0, tiled=True)
    event_types = lax.all_gather(token_types[:, 0], "type", axis=0, tiled=True)
    hot = (event_types[None, :] == type_ids[:, None]).astype(jnp.int32)
    rank = jnp.cumsum(hot, axis=1) - hot
    place = (
        ((rank[:, None, :] == slot_ids[None, :, None]) & (hot[:, None, :] == 1))
        .astype(jnp.bfloat16)
        .reshape(n_type * EXP_CAP, n_type * tok_rows)
    )
    own_place = lax.dynamic_slice_in_dim(place, my_index * tok_rows, tok_rows, 1)
    contrib = jnp.dot(own_place, tokens, preferred_element_type=jnp.float32).astype(jnp.bfloat16)
    packed = lax.psum_scatter(contrib, "type", scatter_dimension=0, tiled=True)
    block_rows = lax.all_gather(packed, "dp", axis=0, tiled=True)
    gate_act = jnp.dot(block_rows, gate_weight[0], preferred_element_type=jnp.float32)
    up_act = jnp.dot(block_rows, up_weight[0], preferred_element_type=jnp.float32)
    hidden = (jax.nn.silu(gate_act) * up_act).astype(jnp.bfloat16)
    partial_terms = jnp.dot(hidden, down_weight[0], preferred_element_type=jnp.float32)
    summed = lax.psum_scatter(
        partial_terms.astype(jnp.bfloat16), "dp", scatter_dimension=0, tiled=True
    )
    slot_values = lax.all_gather(summed, "type", axis=0, tiled=True)
    expert_out = jnp.einsum(
        "pt,pd->td", own_place, slot_values, preferred_element_type=jnp.float32
    ).astype(jnp.bfloat16)
    mask_row = tile_mask[0, 0]
    allowed = jnp.repeat(mask_row == 1, tok_rows)
    head_count = feat_width // HEAD
    query_heads = queries.reshape(tok_rows, head_count, HEAD)
    key_heads = keys_all.reshape(-1, head_count, HEAD)
    value_heads = slot_values.reshape(-1, head_count, HEAD)
    scores = jnp.einsum(
        "qhd,khd->hqk", query_heads, key_heads, preferred_element_type=jnp.float32
    ) * (1.0 / math.sqrt(HEAD))
    masked = jnp.where(allowed[None, None, :], scores, -jnp.inf)
    row_max = jnp.max(masked, axis=-1, keepdims=True)
    weights = jnp.where(allowed[None, None, :], jnp.exp(masked - row_max), 0.0).astype(jnp.bfloat16)
    total_weight = jnp.sum(weights.astype(jnp.float32), axis=-1)
    slot_weights = jnp.einsum(
        "hqk,pk->hqp", weights, place, preferred_element_type=jnp.float32
    ).astype(jnp.bfloat16)
    attended = (
        jnp.einsum("hqp,phd->qhd", slot_weights, value_heads, preferred_element_type=jnp.float32)
        / jnp.transpose(total_weight)[:, :, None]
    )
    return (expert_out, attended.reshape(tok_rows, feat_width).astype(jnp.bfloat16))


def solution(mesh):
    return jax.shard_map(
        on_device,
        mesh=mesh,
        in_specs=(
            P(("dp", "type"), None),
            P(("dp", "type"), None),
            P("dp", "type", None),
            P(("dp", "type"), None),
            P(("dp", "type"), None),
            P("type", None, "dp"),
            P("type", None, "dp"),
            P("type", "dp", None),
        ),
        out_specs=(P(("dp", "type"), None), P(("dp", "type"), None)),
        check_vma=False,
    )
```

profile of v0, /device:TPU:2, one launch (start us, length us, event | category | flops | bytes accessed | tf_op | source)
XLA Modules:
  0.0 382.4 jit_solution(15770409194891240785)
XLA Ops:
  7.2 0.0 reduce-scatter.3.cloned.1.call-start
  7.2 19.4 %all-gather = s32[1024,1]{0,1:T(1,128)S(1)} all-gather(s32[128,1]{0,1:T(1,128)} %param.9), channel_id=2, replica_groups=mesh['dp'=32,'type'=8] {'type'}, dimensions={0}, use_global_device_ids=true | all-gather | bytes 4608 | tf_op jit(solution)/shard_map/all_gather | solution.py:19
  26.7 0.1 eq.76
  26.8 2.3 reduce-window.6
  29.1 0.3 slice_reduce_fusion
  29.3 0.2 reduce-window.9
  29.5 0.1 add_bitcast_fusion
  29.6 0.2 fusion.22
  29.8 2.6 convolution_convert_fusion.2
  32.4 0.0 reduce-scatter.3.cloned.1.call-update
  32.4 0.0 all-gather.5.cloned.1.call-start
  32.5 37.2 %reduce-scatter.3.cloned.1.call-done = bf16[16,4096]{1,0:T(8,128)(2,1)} async-done(((bf16[128,4096]{1,0:T(8,128)(2,1)}), bf16[16,4096]{1,0:T(8,128)(2,1)}) %reduce-scatter.3.cloned.1.call-update) | async-done | bytes 131088 | tf_op jit(solution)/shard_map/reduce_scatter | solution.py:29
  69.7 0.0 all-gather.5.cloned.1.call-update
  69.7 0.0 reduce-scatter.5.cloned.1.call-start
  69.8 51.9 %all-gather.5.cloned.1.call-done = bf16[512,4096]{1,0:T(8,128)(2,1)} async-done(((bf16[16,4096]{1,0:T(8,128)(2,1)}), bf16[512,4096]{1,0:T(8,128)(2,1)}) %all-gather.5.cloned.1.call-update) | async-done | bytes 4194320 | tf_op jit(solution)/shard_map/all_gather | solution.py:30
  121.7 4.2 %fusion.9 = f32[512,224]{0,1:T(8,128)S(1)} fusion(bf16[512,4096]{1,0:T(8,128)(2,1)} %all-gather.5.cloned.1.call-done, bf16[1,4096,224]{1,2,0:T(8,128)(2,1)} %param.13), kind=kOutput, calls=%fused_computation.16 | convolution fusion | flops 939524096 | bytes 6488064 | tf_op jit(solution)/shard_map/dot_general | solution.py:31
  125.9 7.4 %convolution_convert_fusion = bf16[512,4096]{1,0:T(8,128)(2,1)} fusion(bf16[1,224,4096]{2,1,0:T(8,128)(2,1)S(1)} %copy-done, bf16[512,4096]{1,0:T(8,128)(2,1)} %all-gather.5.cloned.1.call-done, bf16[1,4096,224]{1,2,0:T(8,128)(2,1)} %param.14, f32[512,224]{0,1:T(8,128)S(1)} %fusion.9), kind=kOutput, calls=%fused_computation.8 | convolution fusion | flops 1881833472 | bytes 12517376 | tf_op jit(solution)/shard_map/dot_general | solution.py:34
  133.3 0.0 reduce-scatter.5.cloned.1.call-update
  133.3 0.0 all-gather.9.cloned.1.call-start
  133.4 2.3 copy.13
  135.7 0.0 all-gather.9.cloned.1.call-update
  135.7 0.2 all-gather.7.cloned.1.call-start
  136.0 0.1 broadcast_bitcast_fusion
  136.1 86.8 %reduce-scatter.5.cloned.1.call-done = bf16[16,4096]{1,0:T(8,128)(2,1)} async-done(((bf16[512,4096]{1,0:T(8,128)(2,1)}), bf16[16,4096]{1,0:T(8,128)(2,1)}) %reduce-scatter.5.cloned.1.call-update) | async-done | bytes 131088 | tf_op jit(solution)/shard_map/reduce_scatter | solution.py:35
  222.9 100.8 %all-gather.9.cloned.1.call-done = bf16[1024,4096]{0,1:T(8,128)(2,1)} async-done(((bf16[128,4096]{0,1:T(8,128)(2,1)}), bf16[1024,4096]{0,1:T(8,128)(2,1)}) %all-gather.9.cloned.1.call-update) | async-done | bytes 8388624 | tf_op jit(solution)/shard_map/all_gather | solution.py:18
  323.7 11.4 %fusion.19 = f32[32,128,1024]{2,1,0:T(8,128)} fusion(bf16[1024,32,128]{0,2,1:T(8,128)(2,1)} %bitcast.58, bf16[128,4096]{1,0:T(8,128)(2,1)S(1)} %copy-done.2), kind=kOutput, calls=%fused_computation.21 | convolution fusion | flops 1073741824 | bytes 26214400 | tf_op jit(solution)/shard_map/qhd,khd->hqk/dot_general | solution.py:48
  335.1 18.0 %convert_reduce_fusion = (f32[32,128]{1,0:T(8,128)S(1)}, bf16[32,128,1024]{2,1,0:T(8,128)(2,1)}) fusion(f32[32,128,1024]{2,1,0:T(8,128)} %fusion.19, pred[1024]{0:T(1024)(128)(4,1)S(1)} %broadcast_bitcast_fusion), kind=kOutput, calls=%fused_computation.1 | output fusion | flops 37749760 | bytes 25183232 | tf_op jit(solution)/shard_map/sub | solution.py:53
  353.1 8.8 %all-gather.7.cloned.1.call-done = bf16[128,4096]{1,0:T(8,128)(2,1)} async-done(((bf16[16,4096]{1,0:T(8,128)(2,1)}), bf16[128,4096]{1,0:T(8,128)(2,1)}) %all-gather.7.cloned.1.call-update) | async-done | bytes 1048592 | tf_op jit(solution)/shard_map/all_gather | solution.py:38
  361.9 2.3 copy.19
  364.2 8.0 %fusion.5 = bf16[128,32,128]{0,2,1:T(8,128)(2,1)} fusion(bf16[128,32,128]{0,2,1:T(8,128)(2,1)} %bitcast.59, bf16[32,128,1024]{2,1,0:T(8,128)(2,1)} %get-tuple-element.7, f32[128,32]{0,1:T(8,128)S(1)} %bitcast.65, pred[128,1024]{1,0:T(32,128)(4,1)S(1)} %fusion.22), kind=kOutput, calls=%fused_computation.12 | convolution fusion | flops 1209532416 | bytes 10633216 | tf_op jit(solution)/shard_map/hqp,phd->qhd/dot_general | solution.py:59
  372.2 2.3 copy.17
  374.4 1.5 convolution_convert_fusion.1
  (14 shorter events, 0.1 us)
Async XLA Ops:
  7.2 118.7 %copy-start = (bf16[1,224,4096]{2,1,0:T(8,128)(2,1)S(1)}, bf16[1,224,4096]{2,1,0:T(8,128)(2,1)}, u32[]{:S(2)}) copy-start(bf16[1,224,4096]{2,1,0:T(8,128)(2,1)} %param.15) | copy-start | bytes 5505028
  7.2 62.5 %reduce-scatter.3.cloned.1.call-start = ((), (), s32[]{:S(2)}) async-start(), calls=%async_computation.2 | async-start | bytes 1179648 | tf_op jit(solution)/shard_map/reduce_scatter | solution.py:29
  32.4 89.2 %all-gather.5.cloned.1.call-start = ((), (), s32[]{:S(2)}) async-start(), calls=%async_computation.3 | async-start | bytes 4325376 | tf_op jit(solution)/shard_map/all_gather | solution.py:30
  69.7 153.1 %reduce-scatter.5.cloned.1.call-start = ((), (), s32[]{:S(2)}) async-start(), calls=%async_computation.4 | async-start | bytes 4325376 | tf_op jit(solution)/shard_map/reduce_scatter | solution.py:35
  133.3 2.7 copy-start.3
  133.3 190.4 %copy-start.2 = (bf16[128,4096]{1,0:T(8,128)(2,1)S(1)}, bf16[128,4096]{1,0:T(8,128)(2,1)}, u32[]{:S(2)}) copy-start(bf16[128,4096]{1,0:T(8,128)(2,1)} %param.11) | copy-start | bytes 3145732
  133.3 190.4 %all-gather.9.cloned.1.call-start = ((), (), s32[]{:S(2)}) async-start(), calls=%async_computation.6 | async-start | bytes 9437184 | tf_op jit(solution)/shard_map/all_gather | solution.py:18
  135.7 226.2 %all-gather.7.cloned.1.call-start = ((), (), s32[]{:S(2)}) async-start(), calls=%async_computation.5 | async-start | bytes 1179648 | tf_op jit(solution)/shard_map/all_gather | solution.py:38
  364.2 10.2 %copy-start.1 = (bf16[128,4096]{1,0:T(8,128)(2,1)S(1)}, bf16[128,4096]{1,0:T(8,128)(2,1)}, u32[]{:S(2)}) copy-start(bf16[128,4096]{1,0:T(8,128)(2,1)} %all-gather.7.cloned.1.call-done) | copy-start | bytes 3145732
Sparse Core Ops, SparseCore 0:
  32.6 37.1 reduce-scatter.2
  72.3 49.3 all-gather.4
  133.4 89.3 reduce-scatter.4
  225.0 98.6 all-gather.8
  325.3 36.5 all-gather.6
where the time goes:
time: 383 us; the launch traced here: 382 us
  waiting for transfers between devices  286 us (75%)
  matrix products  35.1 us (9%)
  other arithmetic  20.7 us (5%)
  blocking collectives  19.4 us (5%)
  between operations  13.9 us (4%)
  local copies, waits for them, and re-layouts  7.32 us (2%)
    all_gather x1, waiting for transfers between devices, on_device(): keys_all = lax.all_gather(keys, 'type', axis=0, tiled=True)  101 us
    reduce_scatter x1, waiting for transfers between devices, on_device(): lax.psum_scatter(partial_terms.astype(jnp.bfloat16), 'dp', scatter_dimens...  86.8 us
    all_gather x1, waiting for transfers between devices, on_device(): block_rows = lax.all_gather(packed, 'dp', axis=0, tiled=True)  51.9 us
    reduce_scatter x1, waiting for transfers between devices, on_device(): packed = lax.psum_scatter(contrib, 'type', scatter_dimension=0, tiled=True)  37.2 us
    all_gather x1, blocking collectives, on_device(): event_types = lax.all_gather(token_types[:, 0], 'type', axis=0, tiled=True)  19.4 us
    sub x1, other arithmetic, on_device(): masked - row_max  18 us
    dot_general x1, matrix products, on_device(): jnp.einsum('qhd,khd->hqk', query_heads, key_heads, preferred_element_type...  11.4 us
    all_gather x1, waiting for transfers between devices, on_device(): slot_values = lax.all_gather(summed, 'type', axis=0, tiled=True)  8.81 us
  transfers between devices with their start and end apart: 5, of which 5 were waited for; matrix products, arithmetic and copies ran while one was open for 8% of the time, Pallas kernels for 0%

commit v1 on v0

--- a/solution.py
+++ b/solution.py
@@ -35,7 +35,9 @@
     summed = lax.psum_scatter(
         partial_terms.astype(jnp.bfloat16), "dp", scatter_dimension=0, tiled=True
     )
-    slot_values = lax.all_gather(summed, "type", axis=0, tiled=True)
+    slot_values = jnp.concatenate(
+        lax.all_to_all(jnp.stack([summed] * lax.axis_size("type")), "type", 0, 0), axis=0
+    )
     expert_out = jnp.einsum(
         "pt,pd->td", own_place, slot_values, preferred_element_type=jnp.float32
     ).astype(jnp.bfloat16)

time: 383 us -> 389 us (1.016)
  starting transfers between devices: 0.38 us -> 7.19 us
    all_gather x1, waiting for transfers between devices: 101 us -> 110 us  [on_device(): keys_all = lax.all_gather(keys, 'type', axis=0, tiled=True)]
    all_gather x1 -> x0, waiting for transfers between devices: 8.81 us -> none  [on_device(): slot_values = lax.all_gather(summed, 'type', axis=0, tiled=True)]
    all_to_all x0 -> x1, starting transfers between devices: none -> 7.03 us  [on_device(): lax.all_to_all(jnp.stack([summed] * lax.axis_size('type')), 'type', 0, 0)]
  transfers between devices with their start and end apart: 5 -> 5, of which waited for: 5 -> 4; matrix products, arithmetic and copies ran while one was open for 8% -> 9% of each run, Pallas kernels for 0% -> 0%
where the time goes in v1:
time: 389 us
  waiting for transfers between devices  286 us (74%)
  matrix products  34.4 us (9%)
  other arithmetic  20.7 us (5%)
  blocking collectives  19.4 us (5%)
  between operations  13.9 us (4%)
  local copies, waits for them, and re-layouts  7.38 us (2%)
  starting transfers between devices  7.19 us (2%)
    all_gather x1, waiting for transfers between devices, on_device(): keys_all = lax.all_gather(keys, 'type', axis=0, tiled=True)  110 us
    reduce_scatter x1, waiting for transfers between devices, on_device(): lax.psum_scatter(partial_terms.astype(jnp.bfloat16), 'dp', scatter_dimens...  86.9 us
    all_gather x1, waiting for transfers between devices, on_device(): block_rows = lax.all_gather(packed, 'dp', axis=0, tiled=True)  51.9 us
    reduce_scatter x1, waiting for transfers between devices, on_device(): packed = lax.psum_scatter(contrib, 'type', scatter_dimension=0, tiled=True)  37.2 us
    all_gather x1, blocking collectives, on_device(): event_types = lax.all_gather(token_types[:, 0], 'type', axis=0, tiled=True)  19.4 us
    sub x1, other arithmetic, on_device(): masked - row_max  18 us
    dot_general x1, matrix products, on_device(): jnp.einsum('qhd,khd->hqk', query_heads, key_heads, preferred_element_type...  11.8 us
  transfers between devices with their start and end apart: 5, of which 4 were waited for; matrix products, arithmetic and copies ran while one was open for 9% of the time, Pallas kernels for 0%

profile of v1, /device:TPU:2, one launch (start us, length us, event | category | flops | bytes accessed | tf_op | source)
XLA Modules:
  0.0 389.0 jit_solution(8195526194786602625)
XLA Ops:
  7.2 0.0 reduce-scatter.3.cloned.1.call-start
  7.2 19.4 %all-gather = s32[1024,1]{0,1:T(1,128)S(1)} all-gather(s32[128,1]{0,1:T(1,128)} %param.9), channel_id=2, replica_groups=mesh['dp'=32,'type'=8] {'type'}, dimensions={0}, use_global_device_ids=true | all-gather | bytes 4608 | tf_op jit(solution)/shard_map/all_gather | solution.py:19
  26.7 0.1 eq.76
  26.8 2.3 reduce-window.6
  29.1 0.3 slice_reduce_fusion
  29.3 0.2 reduce-window.9
  29.5 0.1 add_bitcast_fusion
  29.6 0.2 fusion.23
  29.8 2.6 convolution_convert_fusion.2
  32.4 0.0 reduce-scatter.3.cloned.1.call-update
  32.4 0.0 all-gather.4.cloned.1.call-start
  32.5 37.2 %reduce-scatter.3.cloned.1.call-done = bf16[16,4096]{1,0:T(8,128)(2,1)} async-done(((bf16[128,4096]{1,0:T(8,128)(2,1)}), bf16[16,4096]{1,0:T(8,128)(2,1)}) %reduce-scatter.3.cloned.1.call-update) | async-done | bytes 131088 | tf_op jit(solution)/shard_map/reduce_scatter | solution.py:29
  69.7 0.0 all-gather.4.cloned.1.call-update
  69.7 0.0 reduce-scatter.5.cloned.1.call-start
  69.8 51.9 %all-gather.4.cloned.1.call-done = bf16[512,4096]{1,0:T(8,128)(2,1)} async-done(((bf16[16,4096]{1,0:T(8,128)(2,1)}), bf16[512,4096]{1,0:T(8,128)(2,1)}) %all-gather.4.cloned.1.call-update) | async-done | bytes 4194320 | tf_op jit(solution)/shard_map/all_gather | solution.py:30
  121.7 4.2 %fusion.9 = f32[512,224]{0,1:T(8,128)S(1)} fusion(bf16[512,4096]{1,0:T(8,128)(2,1)} %all-gather.4.cloned.1.call-done, bf16[1,4096,224]{1,2,0:T(8,128)(2,1)} %param.13), kind=kOutput, calls=%fused_computation.16 | convolution fusion | flops 939524096 | bytes 6488064 | tf_op jit(solution)/shard_map/dot_general | solution.py:31
  125.9 7.4 %convolution_convert_fusion = bf16[512,4096]{1,0:T(8,128)(2,1)} fusion(bf16[1,224,4096]{2,1,0:T(8,128)(2,1)S(1)} %copy-done, bf16[512,4096]{1,0:T(8,128)(2,1)} %all-gather.4.cloned.1.call-done, bf16[1,4096,224]{1,2,0:T(8,128)(2,1)} %param.14, f32[512,224]{0,1:T(8,128)S(1)} %fusion.9), kind=kOutput, calls=%fused_computation.8 | convolution fusion | flops 1881833472 | bytes 12517376 | tf_op jit(solution)/shard_map/dot_general | solution.py:34
  133.3 0.0 reduce-scatter.5.cloned.1.call-update
  133.3 0.0 all-gather.6.cloned.1.call-start
  133.4 1.1 copy-done.1
  134.5 1.3 copy.13
  135.9 0.1 broadcast_bitcast_fusion
  135.9 86.9 %reduce-scatter.5.cloned.1.call-done = bf16[16,4096]{1,0:T(8,128)(2,1)} async-done(((bf16[512,4096]{1,0:T(8,128)(2,1)}), bf16[16,4096]{1,0:T(8,128)(2,1)}) %reduce-scatter.5.cloned.1.call-update) | async-done | bytes 131088 | tf_op jit(solution)/shard_map/reduce_scatter | solution.py:35
  222.9 2.0 stack.2
  224.8 7.0 %all-to-all-start = ((bf16[8,16,4096]{2,1,0:T(8,128)(2,1)}), bf16[8,16,4096]{2,1,0:T(8,128)(2,1)S(1)}, u32[]{:S(2)}, u32[]{:S(2)}) async-start(bf16[8,16,4096]{2,1,0:T(8,128)(2,1)} %stack.2), calls=%async_computation.2 | async-start | bytes 2097152 | tf_op jit(solution)/shard_map/all_to_all | solution.py:39
  231.9 110.0 %all-gather.6.cloned.1.call-done = bf16[1024,4096]{0,1:T(8,128)(2,1)} async-done(((bf16[128,4096]{0,1:T(8,128)(2,1)}), bf16[1024,4096]{0,1:T(8,128)(2,1)}) %all-gather.6.cloned.1.call-update) | async-done | bytes 8388624 | tf_op jit(solution)/shard_map/all_gather | solution.py:18
  341.8 11.8 %fusion.19 = f32[32,128,1024]{2,1,0:T(8,128)} fusion(bf16[1024,32,128]{0,2,1:T(8,128)(2,1)} %bitcast.60, bf16[128,4096]{1,0:T(8,128)(2,1)} %param.11), kind=kOutput, calls=%fused_computation.21 | convolution fusion | flops 1073741824 | bytes 26214400 | tf_op jit(solution)/shard_map/qhd,khd->hqk/dot_general | solution.py:50
  353.6 18.0 %convert_reduce_fusion = (f32[32,128]{1,0:T(8,128)S(1)}, bf16[32,128,1024]{2,1,0:T(8,128)(2,1)}) fusion(f32[32,128,1024]{2,1,0:T(8,128)} %fusion.19, pred[1024]{0:T(1024)(128)(4,1)S(1)} %broadcast_bitcast_fusion), kind=kOutput, calls=%fused_computation.1 | output fusion | flops 37749760 | bytes 25183232 | tf_op jit(solution)/shard_map/sub | solution.py:55
  371.6 1.5 convolution_convert_fusion.1
  373.0 1.2 copy.21
  374.2 6.9 %fusion.5 = bf16[128,32,128]{0,2,1:T(8,128)(2,1)S(1)} fusion(bf16[32,128,1024]{2,1,0:T(8,128)(2,1)} %get-tuple-element.7, bf16[128,32,128]{2,1,0:T(8,128)(2,1)} %bitcast.63, f32[128,32]{0,1:T(8,128)S(1)} %bitcast.69, pred[128,1024]{1,0:T(32,128)(4,1)S(1)} %fusion.23), kind=kOutput, calls=%fused_computation.12 | convolution fusion | flops 1209532416 | bytes 10633216 | tf_op jit(solution)/shard_map/hqp,phd->qhd/dot_general | solution.py:61
  381.1 1.3 copy.17
  (12 shorter events, 0.1 us)
Async XLA Ops:
  7.2 118.7 %copy-start = (bf16[1,224,4096]{2,1,0:T(8,128)(2,1)S(1)}, bf16[1,224,4096]{2,1,0:T(8,128)(2,1)}, u32[]{:S(2)}) copy-start(bf16[1,224,4096]{2,1,0:T(8,128)(2,1)} %param.15) | copy-start | bytes 5505028
  7.2 62.5 %reduce-scatter.3.cloned.1.call-start = ((), (), s32[]{:S(2)}) async-start(), calls=%async_computation.3 | async-start | bytes 1179648 | tf_op jit(solution)/shard_map/reduce_scatter | solution.py:29
  32.4 89.2 %all-gather.4.cloned.1.call-start = ((), (), s32[]{:S(2)}) async-start(), calls=%async_computation.4 | async-start | bytes 4325376 | tf_op jit(solution)/shard_map/all_gather | solution.py:30
  69.7 153.1 %reduce-scatter.5.cloned.1.call-start = ((), (), s32[]{:S(2)}) async-start(), calls=%async_computation.5 | async-start | bytes 4325376 | tf_op jit(solution)/shard_map/reduce_scatter | solution.py:35
  133.3 1.2 copy-start.1
  133.3 2.5 copy-start.2
  133.3 208.5 %all-gather.6.cloned.1.call-start = ((), (), s32[]{:S(2)}) async-start(), calls=%async_computation.6 | async-start | bytes 9437184 | tf_op jit(solution)/shard_map/all_gather | solution.py:18
  224.8 146.7 %all-to-all-start = ((bf16[8,16,4096]{2,1,0:T(8,128)(2,1)}), bf16[8,16,4096]{2,1,0:T(8,128)(2,1)S(1)}, u32[]{:S(2)}, u32[]{:S(2)}) async-start(bf16[8,16,4096]{2,1,0:T(8,128)(2,1)} %stack.2), calls=%async_computation.2 | async-start | bytes 2097152 | tf_op jit(solution)/shard_map/all_to_all | solution.py:39
Sparse Core Ops, SparseCore 0:
  32.6 37.1 reduce-scatter.2
  72.3 49.3 all-gather.3
  133.4 89.3 reduce-scatter.4
  225.0 116.7 all-gather.5
